TPU v7x, 32 devices: a whole 2x2x4 slice. The times are simulated.
32 devices in a mesh: old: 4 (over y, core), new: 8 (over z, x).
Axes of the slice: x: 2, y: 2, z: 4, core: 2. Of those that a mesh axis runs over, the one named last changes fastest.
Arguments:
- old_field: bfloat16 [3, 27, 98304], P(None, None, ('old', 'new')), may hold values from -6 to 6
- pair_dest: int32 [32768, 1], P(('old', 'new')), may hold values from 0 to 31; in each aligned block of 1024 rows (0 to 1023, 1024 to 2047, ...) at most 128 rows name the same one
- pair_new: int32 [32768], P(('old', 'new')), may hold values from 0 to 511
- pair_old: int32 [32768], P(('old', 'new')), may hold values from 0 to 3071
- pair_block: int32 [32768], P(('old', 'new')), may hold values from 0 to 3
- basis_old: bfloat16 [4, 27, 125], replicated, may hold values from -1.25 to 1.25
- basis_new: bfloat16 [4, 27, 125], replicated, may hold values from -0.5 to 0.5
- volume: float32 [2, 8, 1024], P(None, 'old', 'new'), may hold values from 0.25 to 36, as said below
Outputs:
- solution: float32 [3, 5, 16, 2048], P(None, None, 'old', 'new')
- residual: float32 [3, 5, 16, 2048], P(None, None, 'old', 'new')
Inputs may be any that keep to these rules, and one draw needn't show every extreme that they name: `pair_dest`: a device's index is its position along old times the number of devices along new plus its position along new; in each device's block of 1024 pairs at most 128 name one destination. `pair_new`: local element number (x * 2 + y) * 128 + z within the destination's block. `pair_old`: old element within the block of the device that holds the pair. `volume`: positive element factors.
All inputs are finite; a program needn't handle non-finite values.
Results may differ from a plain program's by a relative error of at most 0.003.
Values may be sent and summed in bfloat16 or wider, within the bound.
A program may use at most 64 MiB of HBM per device.

v0:
```python
import jax
import jax.numpy as jnp
import numpy as np
from jax import lax
from jax.sharding import PartitionSpec as P

ITERS = 4
LINE_MASS = np.array([[4.0, 2.0, -1.0], [2.0, 16.0, 2.0], [-1.0, 2.0, 4.0]]) / 15.0


def passed_along(shard, axis, by):
    size = lax.axis_size(axis)
    return lax.ppermute(shard, axis, [(i, (i + by) % size) for i in range(size)])


def split_axis(array, axis, count):
    moved = jnp.moveaxis(array, axis, -1)
    paired = moved[..., : 2 * count].reshape(moved.shape[:-1] + (count, 2))
    even_nodes = paired[..., 0]
    odd_nodes = paired[..., 1]
    after_nodes = jnp.concatenate(
        [even_nodes[..., 1:], moved[..., 2 * count : 2 * count + 1]], axis=-1
    )
    stacked = jnp.stack([even_nodes, odd_nodes, after_nodes], axis=0)
    return jnp.moveaxis(stacked, -1, axis + 1)


def pick_nodes(extended, cell_counts):
    along_first, along_second, along_third = cell_counts
    stacked = split_axis(extended, 3, along_third)
    stacked = split_axis(stacked, 3, along_second)
    stacked = split_axis(stacked, 3, along_first)
    return jnp.transpose(stacked, (3, 0, 1, 2, 4, 5, 6))


def merge_axis(array, local_axis, cell_axis):
    moved = jnp.moveaxis(array, (local_axis, cell_axis), (0, -1))
    count = moved.shape[-1]
    zero_pad = [(0, 0)] * (moved.ndim - 2)
    even_full = jnp.pad(moved[0], zero_pad + [(0, 1)]) + jnp.pad(moved[2], zero_pad + [(1, 0)])
    woven = jnp.stack([even_full[..., :count], moved[1]], axis=-1)
    woven = woven.reshape(woven.shape[:-2] + (2 * count,))
    return jnp.concatenate([woven, even_full[..., count:]], axis=-1)


def spread_nodes(element_nodes):
    summed = merge_axis(element_nodes, 3, 6)
    summed = merge_axis(summed, 2, 4)
    summed = merge_axis(summed, 1, 2)
    return jnp.transpose(summed, (0, 3, 2, 1))


def element_mass(element_nodes, volume):
    line_mass = jnp.asarray(LINE_MASS, dtype=jnp.float32)
    high = lax.Precision.HIGHEST
    applied = jnp.einsum("ia,cabdxyz->cibdxyz", line_mass, element_nodes, precision=high)
    applied = jnp.einsum("jb,cibdxyz->cijdxyz", line_mass, applied, precision=high)
    applied = jnp.einsum("kd,cijdxyz->cijkxyz", line_mass, applied, precision=high)
    return applied * volume


def fold_rims(assembled):
    front_face = passed_along(assembled[..., -1], "new", 1)
    inner_part = assembled[..., :-1]
    inner_part = jnp.concatenate(
        [inner_part[..., :1] + front_face[..., None], inner_part[..., 1:]], axis=3
    )
    side_face = passed_along(inner_part[:, :, -1, :], "old", 1)
    folded = inner_part[:, :, :-1]
    folded = jnp.concatenate(
        [folded[:, :, :1] + side_face[:, :, None, :], folded[:, :, 1:]], axis=2
    )
    return folded


def operate(vector, volume):
    upper_layer = passed_along(vector[..., 0], "new", -1)
    extended = jnp.concatenate([vector, upper_layer[..., None]], axis=3)
    upper_row = passed_along(extended[:, :, 0, :], "old", -1)
    extended = jnp.concatenate([extended, upper_row[:, :, None, :]], axis=2)
    element_nodes = pick_nodes(extended, volume.shape)
    return fold_rims(spread_nodes(element_mass(element_nodes, volume)))


def quadrature(coefficients, block_kind, basis_old, basis_new):
    summed = jnp.zeros(coefficients.shape, jnp.float32)
    for q in range(basis_old.shape[0]):
        chosen = jnp.where(
            (block_kind == q)[None, None, :], coefficients, jnp.zeros((), coefficients.dtype)
        )
        values = jnp.einsum(
            "cap,ak->ckp", chosen, basis_old[q], preferred_element_type=jnp.float32
        ).astype(jnp.bfloat16)
        summed = summed + jnp.einsum(
            "ckp,ak->cap", values, basis_new[q], preferred_element_type=jnp.float32
        )
    return summed


def squares(residual):
    return lax.psum(jnp.sum(residual * residual, axis=(1, 2, 3)), ("old", "new"))


def on_device(old_field, pair_dest, pair_new, pair_old, pair_block, basis_old, basis_new, volume):
    devices = lax.axis_size(("old", "new"))
    pair_count = pair_dest.shape[0]
    capacity = 4 * pair_count // devices
    cells_one, cells_two, cells_three = volume.shape
    elements = cells_one * cells_two * cells_three
    destination = pair_dest[:, 0]
    onehot = (destination[:, None] == jnp.arange(devices, dtype=jnp.int32)[None, :]).astype(
        jnp.int32
    )
    slot_rank = jnp.sum((jnp.cumsum(onehot, axis=0) - onehot) * onehot, axis=1)
    position = destination * capacity + slot_rank
    gathered = jnp.take(old_field, pair_old, axis=2)
    contribution = quadrature(gathered, pair_block, basis_old, basis_new)
    outgoing = (
        jnp.zeros((81, devices * capacity), jnp.float32)
        .at[:, position]
        .set(contribution.reshape(81, -1))
    )
    targets = jnp.full((devices * capacity,), elements, jnp.int32).at[position].set(pair_new)
    received, slot_element = (
        lax.all_to_all(
            outgoing.reshape(81, devices, capacity),
            ("old", "new"),
            split_axis=1,
            concat_axis=1,
            tiled=True,
        ),
        lax.all_to_all(
            targets.reshape(1, devices, capacity),
            ("old", "new"),
            split_axis=1,
            concat_axis=1,
            tiled=True,
        ),
    )
    arrived = received.reshape(81, -1)
    slot_element = slot_element.reshape(-1)
    element_load = (
        jnp.zeros((81, elements + 1), jnp.float32).at[:, slot_element].add(arrived)[:, :elements]
    )
    load_vector = fold_rims(
        spread_nodes(element_load.reshape(3, 3, 3, 3, cells_one, cells_two, cells_three))
    )
    solution = jnp.zeros_like(load_vector)
    residual = load_vector
    direction = load_vector
    norm_now = squares(residual)
    for iteration in range(ITERS):
        applied = operate(direction, volume)
        curvature = lax.psum(jnp.sum(direction * applied, axis=(1, 2, 3)), ("old", "new"))
        step_size = norm_now / curvature
        solution = solution + step_size[:, None, None, None] * direction
        residual = residual - step_size[:, None, None, None] * applied
        norm_next = squares(residual)
        direction = residual + (norm_next / norm_now)[:, None, None, None] * direction
        norm_now = norm_next
    return (solution, residual)


def solution(mesh):
    in_specs = (
        P(None, None, ("old", "new")),
        P(("old", "new"), None),
        P(("old", "new")),
        P(("old", "new")),
        P(("old", "new")),
        P(),
        P(),
        P(None, "old", "new"),
    )
    out_specs = (P(None, None, "old", "new"), P(None, None, "old", "new"))
    return jax.shard_map(
        on_device, mesh=mesh, in_specs=in_specs, out_specs=out_specs, check_vma=False
    )
```

profile of v0, /device:TPU:10, one launch (start us, length us, event | category | flops | bytes accessed | tf_op | source)
XLA Modules:
  0.0 578.3 jit_solution(5909297454449030575)
XLA Ops:
  1.3 9.0 %reduce-window.6 = s32[32,8,128]{2,1,0:T(8,128)S(1)} reduce-window(s32[32,8,128]{2,1,0:T(8,128)S(1)} %fusion.60, s32[]{:T(128)} %constant.17.clone.1), window={size=1x1x128 pad=0_0x0_0x127_0}, to_apply=%region_0.0 | reduce-window | flops 4161536 | bytes 262148 | tf_op jit(solution)/shard_map/reduce-window
  12.3 5.1 scatter_custom_fusion
  17.3 6.0 %all-to-all-start = ((s32[1,32,128]{2,0,1:T(1,128)}), s32[1,32,128]{2,0,1:T(1,128)S(1)}, u32[]{:S(2)}, u32[]{:S(2)}) async-start(s32[1,32,128]{2,0,1:T(1,128)} %bitcast.6), calls=%async_computation | async-start | bytes 32768 | tf_op jit(solution)/shard_map/all_to_all | solution.py:132
  24.8 4.5 copy.623
  30.0 7.5 %gather_fusion = bf16[1024,3,27]{2,1,0:T(4,128)(2,1)} fusion(bf16[3,27,3072]{1,0,2:T(4,128)(2,1)S(1)} %copy.623, s32[1024]{0:T(1024)S(1)} %fusion.106), kind=kCustom, calls=%fused_computation | custom fusion | bytes 335872 | tf_op jit(solution)/shard_map/jit(_take)/gather | solution.py:116
  37.6 9.2 %select_bitcast_fusion.3 = (bf16[3,27,1024]{1,0,2:T(4,128)(2,1)}, bf16[3,27,1024]{1,0,2:T(4,128)(2,1)S(1)}, bf16[3,27,1024]{1,0,2:T(4,128)(2,1)S(1)}, bf16[3,27,1024]{1,0,2:T(4,128)(2,1)S(1)}) fusion(pred[1024]{0:T(1024)(128)(4,1)S(1)} %get-tuple-element.120, bf16[1024,3,27]{2,1,0:T(4,128)(2,1)} %gather_fusion, pred[1024]{0:T(1024)(128)(4,1)S(1)} %get-tuple-element.126, ...), kind=kLoop, calls=%fused_computation.31 | loop fusion | flops 414720 | bytes 834560 | tf_op jit(solution)/shard_map/jit(_where)/select_n | solution.py:88
  48.2 2.3 fusion.5
  53.8 3.8 scatter_custom_fusion.1
  59.3 5.8 %all-to-all-start.1 = ((f32[81,32,128]{2,0,1:T(8,128)}), f32[81,32,128]{2,0,1:T(8,128)S(1)}, u32[]{:S(2)}, u32[]{:S(2)}) async-start(f32[81,32,128]{2,0,1:T(8,128)} %copy.641), calls=%async_computation.1 | async-start | bytes 2883584 | tf_op jit(solution)/shard_map/all_to_all | solution.py:125
  65.8 31.4 %all-to-all-done.1 = f32[81,32,128]{2,0,1:T(8,128)S(1)} async-done(((f32[81,32,128]{2,0,1:T(8,128)}), f32[81,32,128]{2,0,1:T(8,128)S(1)}, u32[]{:S(2)}, u32[]{:S(2)}) %all-to-all-start.1) | async-done | bytes 1327136 | tf_op jit(solution)/shard_map/all_to_all | solution.py:125
  99.4 28.0 %scatter_custom_fusion.2 = f32[81,513]{0,1:T(8,128)S(1)} fusion(s32[4096]{0:T(1024)} %bitcast.616, f32[4096,81]{1,0:T(8,128)S(1)} %copy.643, f32[]{:T(128)} %constant.14.clone.1), kind=kCustom, calls=%fused_computation.113 | custom fusion | flops 331776 | bytes 166724 | tf_op jit(solution)/shard_map/scatter-add | solution.py:143
  128.1 4.3 copy.777
  132.4 6.2 %reshape.241 = f32[3,3,3,2,2,256]{5,4,3,0,1,2:T(2,128)S(1)} reshape(f32[3,3,3,2,2,128,2]{6,5,4,3,0,1,2:T(8,128)} %copy.777) | data formatting | bytes 221184 | tf_op jit(solution)/shard_map/reshape | solution.py:42
  140.1 3.0 collective-permute-done
  143.7 3.0 collective-permute-done.1
  147.0 2.4 collective-permute-start.2
  154.1 2.5 fusion.118
  156.6 2.2 copy.806
  162.4 4.3 copy.779
  166.7 6.2 %reshape.242 = f32[3,3,3,2,2,256]{5,4,3,0,1,2:T(2,128)S(1)} reshape(f32[3,3,3,2,2,128,2]{6,5,4,3,0,1,2:T(8,128)} %copy.779) | data formatting | bytes 221184 | tf_op jit(solution)/shard_map/reshape | solution.py:42
  174.5 3.0 collective-permute-done.4
  178.1 2.9 collective-permute-done.5
  181.4 45.8 %all-reduce.30 = (f32[3]{0:T(128)S(1)}, f32[3]{0:T(128)S(1)}) all-reduce(f32[3]{0:T(128)S(1)} %get-tuple-element.7, f32[3]{0:T(128)S(1)} %get-tuple-element.6), channel_id=1, replica_groups=mesh['old'=4,'new'=8] {'old','new'}, use_global_device_ids=true, to_apply=%region_7.8 | all-reduce | flops 6 | bytes 48 | tf_op jit(solution)/shard_map/psum | solution.py:101
  227.4 38.4 %psum.58 = f32[3]{0:T(128)S(1)} all-reduce(f32[3]{0:T(128)S(1)} %get-tuple-element.20), channel_id=1, replica_groups=mesh['old'=4,'new'=8] {'old','new'}, use_global_device_ids=true, to_apply=%region_11.12 | all-reduce | flops 3 | bytes 24 | tf_op jit(solution)/shard_map/psum | solution.py:101
  266.2 4.5 collective-permute-done.6
  273.4 2.5 fusion.117
  281.7 4.3 copy.781
  286.0 6.2 %reshape.243 = f32[3,3,3,2,2,256]{5,4,3,0,1,2:T(2,128)S(1)} reshape(f32[3,3,3,2,2,128,2]{6,5,4,3,0,1,2:T(8,128)} %copy.781) | data formatting | bytes 221184 | tf_op jit(solution)/shard_map/reshape | solution.py:42
  293.2 3.6 collective-permute-done.8
  297.5 2.8 collective-permute-done.9
  300.6 42.8 %psum.59 = f32[3]{0:T(128)S(1)} all-reduce(f32[3]{0:T(128)S(1)} %get-tuple-element.18), channel_id=1, replica_groups=mesh['old'=4,'new'=8] {'old','new'}, use_global_device_ids=true, to_apply=%region_13.14 | all-reduce | flops 3 | bytes 24 | tf_op jit(solution)/shard_map/psum | solution.py:154
  343.6 39.3 %psum.60 = f32[3]{0:T(128)S(1)} all-reduce(f32[3]{0:T(128)S(1)} %get-tuple-element.16), channel_id=1, replica_groups=mesh['old'=4,'new'=8] {'old','new'}, use_global_device_ids=true, to_apply=%region_15.16 | all-reduce | flops 3 | bytes 24 | tf_op jit(solution)/shard_map/psum | solution.py:101
  383.2 4.5 collective-permute-done.10
  390.7 2.5 fusion.116
  399.0 4.3 copy.783
  403.3 6.2 %reshape.244 = f32[3,3,3,2,2,256]{5,4,3,0,1,2:T(2,128)S(1)} reshape(f32[3,3,3,2,2,128,2]{6,5,4,3,0,1,2:T(8,128)} %copy.783) | data formatting | bytes 221184 | tf_op jit(solution)/shard_map/reshape | solution.py:42
  410.4 3.6 collective-permute-done.12
  414.4 3.2 collective-permute-done.13
  417.9 42.8 %psum.61 = f32[3]{0:T(128)S(1)} all-reduce(f32[3]{0:T(128)S(1)} %get-tuple-element.14), channel_id=1, replica_groups=mesh['old'=4,'new'=8] {'old','new'}, use_global_device_ids=true, to_apply=%region_17.18 | all-reduce | flops 3 | bytes 24 | tf_op jit(solution)/shard_map/psum | solution.py:154
  460.9 38.9 %psum.62 = f32[3]{0:T(128)S(1)} all-reduce(f32[3]{0:T(128)S(1)} %get-tuple-element.12), channel_id=1, replica_groups=mesh['old'=4,'new'=8] {'old','new'}, use_global_device_ids=true, to_apply=%region_19.20 | all-reduce | flops 3 | bytes 24 | tf_op jit(solution)/shard_map/psum | solution.py:101
  500.1 4.5 collective-permute-done.14
  507.3 2.5 fusion.115
  509.8 2.2 copy.824
  515.6 4.3 copy.785
  519.9 6.2 %reshape.245 = f32[3,3,3,2,2,256]{5,4,3,0,1,2:T(2,128)S(1)} reshape(f32[3,3,3,2,2,128,2]{6,5,4,3,0,1,2:T(8,128)} %copy.785) | data formatting | bytes 221184 | tf_op jit(solution)/shard_map/reshape | solution.py:42
  527.1 3.6 collective-permute-done.16
  531.1 3.1 collective-permute-done.17
  534.5 42.8 %psum.63 = f32[3]{0:T(128)S(1)} all-reduce(f32[3]{0:T(128)S(1)} %get-tuple-element.10), channel_id=1, replica_groups=mesh['old'=4,'new'=8] {'old','new'}, use_global_device_ids=true, to_apply=%region_21.22 | all-reduce | flops 3 | bytes 24 | tf_op jit(solution)/shard_map/psum | solution.py:154
  (349 shorter events, 57.4 us)
Async XLA Ops:
  10.8 18.5 %copy-start.2 = (bf16[4,27,125]{2,0,1:T(4,128)(2,1)S(1)}, bf16[4,27,125]{2,0,1:T(4,128)(2,1)}, u32[]{:S(2)}) copy-start(bf16[4,27,125]{2,0,1:T(4,128)(2,1)} %param.17) | copy-start | bytes 81004
  10.8 18.5 %copy-start.3 = (bf16[4,27,125]{2,0,1:T(4,128)(2,1)S(1)}, bf16[4,27,125]{2,0,1:T(4,128)(2,1)}, u32[]{:S(2)}) copy-start(bf16[4,27,125]{2,0,1:T(4,128)(2,1)} %param.18) | copy-start | bytes 81004
  12.3 11.8 %copy-start.5 = (s32[1024,1]{0,1:T(1,128)}, s32[1024,1]{0,1:T(1,128)S(1)}, u32[]{:S(2)}) copy-start(s32[1024,1]{0,1:T(1,128)S(1)} %compare_select_fusion.1) | copy-start | bytes 12292
  17.3 42.0 %all-to-all-start = ((s32[1,32,128]{2,0,1:T(1,128)}), s32[1,32,128]{2,0,1:T(1,128)S(1)}, u32[]{:S(2)}, u32[]{:S(2)}) async-start(s32[1,32,128]{2,0,1:T(1,128)} %bitcast.6), calls=%async_computation | async-start | bytes 32768 | tf_op jit(solution)/shard_map/all_to_all | solution.py:132
  48.2 3.6 copy-start
  59.3 37.9 %all-to-all-start.1 = ((f32[81,32,128]{2,0,1:T(8,128)}), f32[81,32,128]{2,0,1:T(8,128)S(1)}, u32[]{:S(2)}, u32[]{:S(2)}) async-start(f32[81,32,128]{2,0,1:T(8,128)} %copy.641), calls=%async_computation.1 | async-start | bytes 2883584 | tf_op jit(solution)/shard_map/all_to_all | solution.py:125
  139.4 3.7 collective-permute-start
  143.4 3.3 collective-permute-start.1
  147.0 4.6 collective-permute-start.2
  151.7 1.6 collective-permute-start.3
  158.8 1.5 copy-start.1
  159.6 2.4 copy-start.4
  173.8 3.7 collective-permute-start.4
  177.8 3.3 collective-permute-start.5
  266.1 4.6 collective-permute-start.6
  270.9 1.8 collective-permute-start.7
  293.1 3.7 collective-permute-start.8
  297.1 3.3 collective-permute-start.9
  383.2 4.6 collective-permute-start.10
  387.9 2.0 collective-permute-start.11
  410.3 3.7 collective-permute-start.12
  414.3 3.3 collective-permute-start.13
  500.0 4.6 collective-permute-start.14
  504.8 1.8 collective-permute-start.15
  526.9 3.7 collective-permute-start.16
  530.9 3.3 collective-permute-start.17
where the time goes:
time: 588 us; the launch traced here: 578 us
  blocking collectives  291 us (49%)
  local copies, waits for them, and re-layouts  109 us (19%)
  waiting for transfers between devices  85.1 us (14%)
  other arithmetic  59.1 us (10%)
  starting transfers between devices  17.8 us (3%)
  matrix products  13.5 us (2%)
    psum x4, blocking collectives, squares(): lax.psum(jnp.sum(residual * residual, axis=(1, 2, 3)), ('old', 'new'))  162 us
    psum x3, blocking collectives, on_device(): lax.psum(jnp.sum(direction * applied, axis=(1, 2, 3)), ('old', 'new'))  128 us
    ppermute x18, waiting for transfers between devices, passed_along(): lax.ppermute(shard, axis, [(i, (i + by) % size) for i in range(size)])  53.7 us
    reshape x20, local copies, waits for them, and re-layouts, merge_axis(): woven = woven.reshape(woven.shape[:-2] + (2 * count,))  52.6 us
    all_to_all x1, waiting for transfers between devices, on_device(): lax.all_to_all(outgoing.reshape(81, devices, capacity), ('old', 'new'), s...  31.4 us
    scatter-add x1, other arithmetic, on_device(): jnp.zeros((81, elements + 1), jnp.float32).at[:, slot_element].add(arrived)  28 us
    unnamed x39, local copies, waits for them, and re-layouts  16.9 us
  transfers between devices with their start and end apart: 20, of which 19 were waited for; matrix products, arithmetic and copies ran while one was open for 6% of the time, Pallas kernels for 0%

commit v1 on v0

--- a/solution.py
+++ b/solution.py
@@ -6,6 +6,13 @@
 
 ITERS = 4
 LINE_MASS = np.array([[4.0, 2.0, -1.0], [2.0, 16.0, 2.0], [-1.0, 2.0, 4.0]]) / 15.0
+
+
+def exchange_blocks(array, name, split, join):
+    n_dev = lax.axis_size(name)
+    pieces = jnp.stack(jnp.split(array, n_dev, axis=split), axis=0)
+    pieces = lax.all_to_all(pieces, name, split_axis=0, concat_axis=0)
+    return jnp.concatenate(pieces, axis=join)
 
 
 def passed_along(shard, axis, by):
@@ -122,13 +129,7 @@
     )
     targets = jnp.full((devices * capacity,), elements, jnp.int32).at[position].set(pair_new)
     received, slot_element = (
-        lax.all_to_all(
-            outgoing.reshape(81, devices, capacity),
-            ("old", "new"),
-            split_axis=1,
-            concat_axis=1,
-            tiled=True,
-        ),
+        exchange_blocks(outgoing.reshape(81, devices, capacity), ("old", "new"), 1, 1),
         lax.all_to_all(
             targets.reshape(1, devices, capacity),
             ("old", "new"),

time: 588 us -> 615 us (1.046)
  local copies, waits for them, and re-layouts: 109 us -> 139 us
    unnamed x39 -> x108, local copies, waits for them, and re-layouts: 16.9 us -> 47.7 us
  transfers between devices with their start and end apart: 20 -> 20, of which waited for: 19 -> 19; matrix products, arithmetic and copies ran while one was open for 6% -> 11% of each run, Pallas kernels for 0% -> 0%
where the time goes in v1:
time: 615 us; the launch traced here: 605 us
  blocking collectives  291 us (47%)
  local copies, waits for them, and re-layouts  139 us (23%)
  waiting for transfers between devices  83.4 us (14%)
  other arithmetic  57.9 us (9%)
  starting transfers between devices  17.1 us (3%)
  matrix products  13.3 us (2%)
    psum x4, blocking collectives, squares(): lax.psum(jnp.sum(residual * residual, axis=(1, 2, 3)), ('old', 'new'))  162 us
    psum x3, blocking collectives, on_device(): lax.psum(jnp.sum(direction * applied, axis=(1, 2, 3)), ('old', 'new'))  128 us
    ppermute x18, waiting for transfers between devices, passed_along(): lax.ppermute(shard, axis, [(i, (i + by) % size) for i in range(size)])  54.3 us
    reshape x20, local copies, waits for them, and re-layouts, merge_axis(): woven = woven.reshape(woven.shape[:-2] + (2 * count,))  52.6 us
    unnamed x108, local copies, waits for them, and re-layouts  47.7 us
    all_to_all x1, waiting for transfers between devices, exchange_blocks(): pieces = lax.all_to_all(pieces, name, split_axis=0, concat_axis=0)  29.1 us
    scatter-add x1, other arithmetic, on_device(): jnp.zeros((81, elements + 1), jnp.float32).at[:, slot_element].add(arrived)  28.1 us
  transfers between devices with their start and end apart: 20, of which 19 were waited for; matrix products, arithmetic and copies ran while one was open for 11% of the time, Pallas kernels for 0%

profile of v1, /device:TPU:10, one launch (start us, length us, event | category | flops | bytes accessed | tf_op | source)
XLA Modules:
  0.0 605.0 jit_solution(4327116500128814933)
XLA Ops:
  1.4 9.0 %reduce-window.6 = s32[32,8,128]{2,1,0:T(8,128)S(1)} reduce-window(s32[32,8,128]{2,1,0:T(8,128)S(1)} %fusion.60, s32[]{:T(128)} %constant.17.clone.1), window={size=1x1x128 pad=0_0x0_0x127_0}, to_apply=%region_0.0 | reduce-window | flops 4161536 | bytes 262148 | tf_op jit(solution)/shard_map/reduce-window
  12.3 5.1 scatter_custom_fusion
  17.3 6.0 all-to-all-start
  23.4 4.5 copy.654
  28.7 7.5 %gather_fusion = bf16[1024,3,27]{2,1,0:T(4,128)(2,1)} fusion(bf16[3,27,3072]{1,0,2:T(4,128)(2,1)S(1)} %copy.654, s32[1024]{0:T(1024)S(1)} %fusion.106), kind=kCustom, calls=%fused_computation | custom fusion | bytes 335872 | tf_op jit(solution)/shard_map/jit(_take)/gather | solution.py:123
  36.2 9.2 %select_bitcast_fusion.3 = (bf16[3,27,1024]{1,0,2:T(4,128)(2,1)}, bf16[3,27,1024]{1,0,2:T(4,128)(2,1)S(1)}, bf16[3,27,1024]{1,0,2:T(4,128)(2,1)S(1)}, bf16[3,27,1024]{1,0,2:T(4,128)(2,1)S(1)}) fusion(pred[1024]{0:T(1024)(128)(4,1)S(1)} %get-tuple-element.152, bf16[1024,3,27]{2,1,0:T(4,128)(2,1)} %gather_fusion, pred[1024]{0:T(1024)(128)(4,1)S(1)} %get-tuple-element.158, ...), kind=kLoop, calls=%fused_computation.32 | loop fusion | flops 414720 | bytes 834560 | tf_op jit(solution)/shard_map/jit(_where)/select_n | solution.py:95
  46.8 2.3 fusion.5
  52.2 3.8 scatter_custom_fusion.1
  88.3 5.8 all-to-all-start.1
  94.8 29.1 %all-to-all-done.1 = f32[32,81,1,128]{3,2,1,0:T(1,128)S(1)} async-done(((f32[32,81,1,128]{3,2,1,0:T(1,128)}), f32[32,81,1,128]{3,2,1,0:T(1,128)S(1)}, u32[]{:S(2)}, u32[]{:S(2)}) %all-to-all-start.1) | async-done | bytes 1327136 | tf_op jit(solution)/shard_map/all_to_all | solution.py:14
  126.1 28.1 %scatter_custom_fusion.2 = f32[81,513]{0,1:T(8,128)S(1)} fusion(s32[4096]{0:T(1024)} %bitcast.688, f32[4096,81]{1,0:T(8,128)S(1)} %copy.705, f32[]{:T(128)} %constant.14.clone.1), kind=kCustom, calls=%fused_computation.114 | custom fusion | flops 331776 | bytes 166724 | tf_op jit(solution)/shard_map/scatter-add | solution.py:144
  154.9 4.3 copy.839
  159.2 6.2 %reshape.241 = f32[3,3,3,2,2,256]{5,4,3,0,1,2:T(2,128)S(1)} reshape(f32[3,3,3,2,2,128,2]{6,5,4,3,0,1,2:T(8,128)} %copy.839) | data formatting | bytes 221184 | tf_op jit(solution)/shard_map/reshape | solution.py:49
  166.8 3.2 collective-permute-done
  170.5 3.0 collective-permute-done.1
  173.8 2.2 collective-permute-start.2
  176.1 2.3 collective-permute-done.2
  181.0 2.5 fusion.120
  189.3 4.3 copy.841
  193.6 6.2 %reshape.242 = f32[3,3,3,2,2,256]{5,4,3,0,1,2:T(2,128)S(1)} reshape(f32[3,3,3,2,2,128,2]{6,5,4,3,0,1,2:T(8,128)} %copy.841) | data formatting | bytes 221184 | tf_op jit(solution)/shard_map/reshape | solution.py:49
  201.1 3.2 collective-permute-done.4
  205.0 3.0 collective-permute-done.5
  208.2 45.6 %all-reduce.30 = (f32[3]{0:T(128)S(1)}, f32[3]{0:T(128)S(1)}) all-reduce(f32[3]{0:T(128)S(1)} %get-tuple-element.7, f32[3]{0:T(128)S(1)} %get-tuple-element.6), channel_id=1, replica_groups=mesh['old'=4,'new'=8] {'old','new'}, use_global_device_ids=true, to_apply=%region_7.8 | all-reduce | flops 6 | bytes 48 | tf_op jit(solution)/shard_map/psum | solution.py:108
  254.1 38.4 %psum.58 = f32[3]{0:T(128)S(1)} all-reduce(f32[3]{0:T(128)S(1)} %get-tuple-element.20), channel_id=1, replica_groups=mesh['old'=4,'new'=8] {'old','new'}, use_global_device_ids=true, to_apply=%region_11.12 | all-reduce | flops 3 | bytes 24 | tf_op jit(solution)/shard_map/psum | solution.py:108
  292.8 4.5 collective-permute-done.6
  300.0 2.5 fusion.119
  308.3 4.3 copy.843
  312.6 6.2 %reshape.243 = f32[3,3,3,2,2,256]{5,4,3,0,1,2:T(2,128)S(1)} reshape(f32[3,3,3,2,2,128,2]{6,5,4,3,0,1,2:T(8,128)} %copy.843) | data formatting | bytes 221184 | tf_op jit(solution)/shard_map/reshape | solution.py:49
  319.8 3.6 collective-permute-done.8
  324.1 2.9 collective-permute-done.9
  327.2 42.8 %psum.59 = f32[3]{0:T(128)S(1)} all-reduce(f32[3]{0:T(128)S(1)} %get-tuple-element.18), channel_id=1, replica_groups=mesh['old'=4,'new'=8] {'old','new'}, use_global_device_ids=true, to_apply=%region_13.14 | all-reduce | flops 3 | bytes 24 | tf_op jit(solution)/shard_map/psum | solution.py:155
  370.2 39.3 %psum.60 = f32[3]{0:T(128)S(1)} all-reduce(f32[3]{0:T(128)S(1)} %get-tuple-element.16), channel_id=1, replica_groups=mesh['old'=4,'new'=8] {'old','new'}, use_global_device_ids=true, to_apply=%region_15.16 | all-reduce | flops 3 | bytes 24 | tf_op jit(solution)/shard_map/psum | solution.py:108
  409.8 4.5 collective-permute-done.10
  417.1 2.5 fusion.118
  425.4 4.3 copy.845
  429.6 6.2 %reshape.244 = f32[3,3,3,2,2,256]{5,4,3,0,1,2:T(2,128)S(1)} reshape(f32[3,3,3,2,2,128,2]{6,5,4,3,0,1,2:T(8,128)} %copy.845) | data formatting | bytes 221184 | tf_op jit(solution)/shard_map/reshape | solution.py:49
  436.8 3.6 collective-permute-done.12
  440.8 3.2 collective-permute-done.13
  444.3 42.8 %psum.61 = f32[3]{0:T(128)S(1)} all-reduce(f32[3]{0:T(128)S(1)} %get-tuple-element.14), channel_id=1, replica_groups=mesh['old'=4,'new'=8] {'old','new'}, use_global_device_ids=true, to_apply=%region_17.18 | all-reduce | flops 3 | bytes 24 | tf_op jit(solution)/shard_map/psum | solution.py:155
  487.3 38.9 %psum.62 = f32[3]{0:T(128)S(1)} all-reduce(f32[3]{0:T(128)S(1)} %get-tuple-element.12), channel_id=1, replica_groups=mesh['old'=4,'new'=8] {'old','new'}, use_global_device_ids=true, to_apply=%region_19.20 | all-reduce | flops 3 | bytes 24 | tf_op jit(solution)/shard_map/psum | solution.py:108
  526.5 4.5 collective-permute-done.14
  533.8 2.5 fusion.117
  536.2 2.2 copy.918
  542.1 4.3 copy.847
  546.3 6.2 %reshape.245 = f32[3,3,3,2,2,256]{5,4,3,0,1,2:T(2,128)S(1)} reshape(f32[3,3,3,2,2,128,2]{6,5,4,3,0,1,2:T(8,128)} %copy.847) | data formatting | bytes 221184 | tf_op jit(solution)/shard_map/reshape | solution.py:49
  553.5 3.6 collective-permute-done.16
  557.6 3.1 collective-permute-done.17
  561.0 42.8 %psum.63 = f32[3]{0:T(128)S(1)} all-reduce(f32[3]{0:T(128)S(1)} %get-tuple-element.10), channel_id=1, replica_groups=mesh['old'=4,'new'=8] {'old','new'}, use_global_device_ids=true, to_apply=%region_21.22 | all-reduce | flops 3 | bytes 24 | tf_op jit(solution)/shard_map/psum | solution.py:155
  (420 shorter events, 85.8 us)
Async XLA Ops:
  0.6 22.7 %copy-start.6 = (s32[1024]{0:T(1024)S(1)}, s32[1024]{0:T(1024)}, u32[]{:S(2)}) copy-start(s32[1024]{0:T(1024)} %param.15) | copy-start | bytes 12292
  0.6 22.7 %copy-start.8 = (s32[1024]{0:T(1024)S(1)}, s32[1024]{0:T(1024)}, u32[]{:S(2)}) copy-start(s32[1024]{0:T(1024)} %param.16) | copy-start | bytes 12292
  12.3 11.1 %copy-start.7 = (s32[1024,1]{0,1:T(1,128)}, s32[1024,1]{0,1:T(1,128)S(1)}, u32[]{:S(2)}) copy-start(s32[1024,1]{0,1:T(1,128)S(1)} %compare_select_fusion.1) | copy-start | bytes 12292
  17.3 71.0 %all-to-all-start = ((s32[1,32,128]{2,0,1:T(1,128)}), s32[1,32,128]{2,0,1:T(1,128)S(1)}, u32[]{:S(2)}, u32[]{:S(2)}) async-start(s32[1,32,128]{2,0,1:T(1,128)} %bitcast.6), calls=%async_computation | async-start | bytes 32768 | tf_op jit(solution)/shard_map/all_to_all | solution.py:133
  23.4 4.6 copy-start.3
  23.4 4.6 copy-start.4
  46.8 3.7 copy-start
  49.1 1.4 copy-start.1
  88.3 35.6 %all-to-all-start.1 = ((f32[32,81,1,128]{3,2,1,0:T(1,128)}), f32[32,81,1,128]{3,2,1,0:T(1,128)S(1)}, u32[]{:S(2)}, u32[]{:S(2)}) async-start(f32[32,81,1,128]{3,2,1,0:T(1,128)} %constant_dynamic-update-slice_fusion), calls=%async_computation.1 | async-start | bytes 2654208 | tf_op jit(solution)/shard_map/all_to_all | solution.py:14
  166.2 3.7 collective-permute-start
  170.3 3.3 collective-permute-start.1
  173.8 4.6 collective-permute-start.2
  178.6 1.6 collective-permute-start.3
  186.4 0.7 copy-start.2
  186.8 2.0 copy-start.5
  200.6 3.7 collective-permute-start.4
  204.7 3.3 collective-permute-start.5
  292.8 4.6 collective-permute-start.6
  297.5 1.8 collective-permute-start.7
  319.7 3.7 collective-permute-start.8
  323.7 3.3 collective-permute-start.9
  409.8 4.6 collective-permute-start.10
  414.5 1.8 collective-permute-start.11
  436.7 3.7 collective-permute-start.12
  440.7 3.3 collective-permute-start.13
  526.4 4.6 collective-permute-start.14
  531.2 1.9 collective-permute-start.15
  553.4 3.7 collective-permute-start.16
  557.4 3.3 collective-permute-start.17
